TPU v7x, 128 devices: a whole 4x4x4 slice. The times are simulated.
128 devices in a mesh: dp: 32 (over z, x, core), seq: 4 (over y).
Axes of the slice: x: 4, y: 4, z: 4, core: 2. Of those that a mesh axis runs over, the one named last changes fastest.
Arguments:
- queries: bfloat16 [32768, 2560], P(('dp', 'seq')), may hold values from -200 to 200
- keys: bfloat16 [32768, 2560], P(('dp', 'seq')), may hold values from -200 to 200
- values: bfloat16 [32768, 2560], P(('dp', 'seq')), may hold values from -6 to 6
- gain_q: float32 [2560], replicated, may hold values from 0.5 to 1.5
- gain_k: float32 [2560], replicated, may hold values from 0.5 to 1.5
- tile_pairs: int32 [16, 8], replicated, may hold values from 0 to 15, as said below
- tile_lens: int32 [32, 16], P('dp'), may hold values from 40 to 64
- out_grad: bfloat16 [32768, 5120], P(('dp', 'seq')), may hold values from -24 to 24
- w_out: bfloat16 [5120, 2560], P('dp', 'seq'), may hold values from -0.125 to 0.125
Outputs:
- grad_q: bfloat16 [32768, 2560], P(('dp', 'seq'))
- grad_k: bfloat16 [32768, 2560], P(('dp', 'seq'))
- grad_v: bfloat16 [32768, 2560], P(('dp', 'seq'))
- grad_w: float32 [5120, 2560], P('dp', 'seq')
Inputs may be any that keep to these rules, and one draw needn't show every extreme that they name: `tile_pairs`: row a lists 8 different tiles of the window, with tile a first.
All inputs are finite; a program needn't handle non-finite values.
Results may differ from a plain program's by a relative error of at most 0.02.
Values may be sent and summed in bfloat16 or wider, within the bound.
No kernel may reach another device: no remote copies, remote signals or barrier semaphores. Data moves between devices by JAX's collectives and lax.ppermute only.
A program may use at most 128 MiB of HBM per device.

v0:
```python
import math
import jax
import jax.numpy as jnp
from jax import lax
from jax.sharding import PartitionSpec as P

HEAD_DIM = 128
EPS = 1e-06


def multiply(pattern, left, right):
    return jnp.einsum(pattern, left, right, preferred_element_type=jnp.float32)


def normalize(field, gain):
    values_f = field.astype(jnp.float32)
    row_scale = lax.rsqrt(jnp.mean(values_f * values_f, axis=-1, keepdims=True) + EPS)
    return ((values_f * row_scale * gain).astype(jnp.bfloat16), row_scale)


def norm_finish(values_f, row_scale, gated, inner, width):
    return (row_scale * gated - values_f * row_scale**3 * inner / width).astype(jnp.bfloat16)


def tile_attention(query_tiles, key_tiles, value_tiles, grad_tiles, tile_pairs, live_lengths):
    tile_count, tile_rows, head_width = query_tiles.shape
    neighbours = tile_pairs.shape[1]
    factor = 1.0 / math.sqrt(head_width)
    key_near = jnp.take(key_tiles, tile_pairs, axis=0).reshape(
        tile_count, neighbours * tile_rows, head_width
    )
    value_near = jnp.take(value_tiles, tile_pairs, axis=0).reshape(
        tile_count, neighbours * tile_rows, head_width
    )
    near_lengths = jnp.take(live_lengths, tile_pairs, axis=0)
    live = (
        jnp.arange(tile_rows, dtype=jnp.int32)[None, None, :] < near_lengths[:, :, None]
    ).reshape(tile_count, neighbours * tile_rows)
    scores = multiply("aqd,akd->aqk", query_tiles, key_near) * factor
    scores = jnp.where(live[:, None, :], scores, -jnp.inf)
    row_max = jnp.max(scores, axis=-1, keepdims=True)
    weights = jnp.exp(scores - row_max)
    probs = weights / jnp.sum(weights, axis=-1, keepdims=True)
    probs_low = probs.astype(jnp.bfloat16)
    attended = multiply("aqk,akd->aqd", probs_low, value_near).astype(jnp.bfloat16)
    grad_probs = multiply("aqd,akd->aqk", grad_tiles, value_near)
    delta = jnp.sum(probs * grad_probs, axis=-1, keepdims=True)
    grad_scores = (probs * (grad_probs - delta)).astype(jnp.bfloat16)
    grad_query = (multiply("aqk,akd->aqd", grad_scores, key_near) * factor).astype(jnp.bfloat16)
    grad_key_near = multiply("aqk,aqd->akd", grad_scores, query_tiles) * factor
    grad_value_near = multiply("aqk,aqd->akd", probs_low, grad_tiles)
    owners = (
        tile_pairs[:, :, None] == jnp.arange(tile_count, dtype=jnp.int32)[None, None, :]
    ).astype(jnp.float32)
    grad_key = jnp.einsum(
        "anb,antd->btd",
        owners,
        grad_key_near.reshape(tile_count, neighbours, tile_rows, head_width),
        precision=lax.Precision.HIGHEST,
    ).astype(jnp.bfloat16)
    grad_value = jnp.einsum(
        "anb,antd->btd",
        owners,
        grad_value_near.reshape(tile_count, neighbours, tile_rows, head_width),
        precision=lax.Precision.HIGHEST,
    ).astype(jnp.bfloat16)
    return (attended, grad_query, grad_key, grad_value)


def per_device(queries, keys, values, gain_q, gain_k, tile_pairs, tile_lens, out_grad, w_out):
    seq_count = lax.axis_size("seq")
    dp_count = lax.axis_size("dp")
    tok_rows = queries.shape[0]
    width = queries.shape[1]
    local_width = width // seq_count
    clip_rows = tok_rows * seq_count
    tile_count = tile_pairs.shape[0]
    tile_rows = clip_rows // tile_count
    head_count = local_width // HEAD_DIM
    clip_lengths = tile_lens[0]
    query_normed, query_scale = normalize(queries, gain_q)
    key_normed, key_scale = normalize(keys, gain_k)
    query_heads, key_heads, value_heads = (
        lax.all_to_all(query_normed, "seq", split_axis=1, concat_axis=0, tiled=True),
        lax.all_to_all(key_normed, "seq", split_axis=1, concat_axis=0, tiled=True),
        lax.all_to_all(values, "seq", split_axis=1, concat_axis=0, tiled=True),
    )
    cot_all = lax.all_gather(out_grad, "seq", axis=0, tiled=True)
    columns = cot_all
    grad_attended = jnp.dot(
        columns, lax.all_gather(w_out, "dp", axis=0, tiled=True), preferred_element_type=jnp.float32
    ).astype(jnp.bfloat16)

    def split(field):
        return field.reshape(tile_count, tile_rows, head_count, HEAD_DIM).transpose(2, 0, 1, 3)

    def merge(field):
        return field.transpose(1, 2, 0, 3).reshape(clip_rows, local_width)

    def one_head(group):
        return tile_attention(group[0], group[1], group[2], group[3], tile_pairs, clip_lengths)

    attended, grad_qn, grad_kn, grad_vh = lax.map(
        one_head, (split(query_heads), split(key_heads), split(value_heads), split(grad_attended))
    )
    attended = merge(attended)
    grad_qn = merge(grad_qn)
    grad_kn = merge(grad_kn)
    grad_vh = merge(grad_vh)
    columns = cot_all
    grad_w = lax.psum_scatter(
        (
            jnp.einsum("td,te->de", columns, attended, preferred_element_type=jnp.float32)
            / dp_count
        ).astype(jnp.bfloat16),
        "dp",
        scatter_dimension=0,
        tiled=True,
    ).astype(jnp.float32)
    grad_qt, grad_kt, grad_v = (
        lax.all_to_all(grad_qn, "seq", split_axis=0, concat_axis=1, tiled=True),
        lax.all_to_all(grad_kn, "seq", split_axis=0, concat_axis=1, tiled=True),
        lax.all_to_all(grad_vh, "seq", split_axis=0, concat_axis=1, tiled=True),
    )
    query_full = queries.astype(jnp.float32)
    key_full = keys.astype(jnp.float32)
    gated_q = gain_q * grad_qt.astype(jnp.float32)
    gated_k = gain_k * grad_kt.astype(jnp.float32)
    inner_q = jnp.sum(gated_q * query_full, axis=-1, keepdims=True)
    inner_k = jnp.sum(gated_k * key_full, axis=-1, keepdims=True)
    grad_q = norm_finish(query_full, query_scale, gated_q, inner_q, width)
    grad_k = norm_finish(key_full, key_scale, gated_k, inner_k, width)
    return (grad_q, grad_k, grad_v, grad_w)


def solution(mesh):
    return jax.shard_map(
        per_device,
        mesh=mesh,
        in_specs=(
            P(("dp", "seq"), None),
            P(("dp", "seq"), None),
            P(("dp", "seq"), None),
            P(),
            P(),
            P(),
            P("dp", None),
            P(("dp", "seq"), None),
            P("dp", "seq"),
        ),
        out_specs=(
            P(("dp", "seq"), None),
            P(("dp", "seq"), None),
            P(("dp", "seq"), None),
            P("dp", "seq"),
        ),
        check_vma=False,
    )
```

profile of v0, /device:TPU:0, one launch (start us, length us, event | category | flops | bytes accessed | tf_op | source)
XLA Modules:
  0.0 484.7 jit_solution(18076181013758219229)
XLA Ops:
  12.3 4.5 all-to-all-start
  23.3 11.4 %all-to-all-done = bf16[256,4,640]{2,0,1:T(8,128)(2,1)S(1)} async-done(((bf16[256,4,640]{2,0,1:T(8,128)(2,1)}), bf16[256,4,640]{2,0,1:T(8,128)(2,1)S(1)}, u32[]{:S(2)}, u32[]{:S(2)}) %all-to-all-start) | async-done | bytes 1310752 | tf_op jit(solution)/shard_map/all_to_all | solution.py:84
  40.8 14.4 %all-to-all-done.1 = bf16[256,4,640]{2,0,1:T(8,128)(2,1)S(1)} async-done(((bf16[256,4,640]{2,0,1:T(8,128)(2,1)}), bf16[256,4,640]{2,0,1:T(8,128)(2,1)S(1)}, u32[]{:S(2)}, u32[]{:S(2)}) %all-to-all-start.1) | async-done | bytes 1310752 | tf_op jit(solution)/shard_map/all_to_all | solution.py:85
  55.2 4.3 all-to-all-start.2
  67.6 8.1 %all-to-all-done.2 = bf16[256,4,640]{2,0,1:T(8,128)(2,1)} async-done(((bf16[256,4,640]{2,0,1:T(8,128)(2,1)}), bf16[256,4,640]{2,0,1:T(8,128)(2,1)}, u32[]{:S(2)}, u32[]{:S(2)}) %all-to-all-start.2) | async-done | bytes 1310752 | tf_op jit(solution)/shard_map/all_to_all | solution.py:86
  80.3 83.5 %all-gather.3.cloned.1.call-done = bf16[1024,5120]{1,0:T(8,128)(2,1)} async-done(((bf16[256,5120]{1,0:T(8,128)(2,1)}), bf16[1024,5120]{1,0:T(8,128)(2,1)}) %all-gather.3.cloned.1.call-update) | async-done | bytes 10485776 | tf_op jit(solution)/shard_map/all_gather | solution.py:88
  163.8 13.7 %convolution_convert_fusion.1 = bf16[1024,640]{1,0:T(8,128)(2,1)} fusion(bf16[1024,5120]{1,0:T(8,128)(2,1)} %all-gather.3.cloned.1.call-done, bf16[5120,640]{1,0:T(8,128)(2,1)} %all-gather.5.cloned.1.call-done), kind=kOutput, calls=%fused_computation.95 | convolution fusion | flops 6711541760 | bytes 18350080 | tf_op jit(solution)/shard_map/dot_general | solution.py:90
  182.1 182.6 %while.18 = (s32[]{:T(128)}, bf16[5,16,64,128]{3,2,1,0:T(8,128)(2,1)}, bf16[5,16,64,128]{3,2,1,0:T(8,128)(2,1)}, bf16[5,16,64,128]{3,1,2,0:T(8,128)(2,1)}, bf16[...) while((s32[]{:T(128)}, ...), condition=%wide.region_6.8_spmd, body=%wide.region_2.7_spmd.sunk | while | flops 1219638656 | bytes 88276472 | solution.py:103
  187.9 4.0 broadcast_select_fusion.6
  204.6 7.3 %fusion.138 = bf16[5,16,64,128]{3,1,2,0:T(8,128)(2,1)} fusion(bf16[5,16,64,128]{3,1,2,0:T(8,128)(2,1)} %get-tuple-element.341, s32[]{:T(128)S(6)} %copy.142, f32[16,8,64,128]{3,2,1,0:T(8,128)} %bitcast.172, s32[16,8]{0,1:T(8,128)S(1)} %copy.132), kind=kOutput, calls=%fused_computation.26.clone.1 | convolution fusion | flops 201459712 | bytes 4456964 | tf_op jit(solution)/shard_map/while/body/eval_jaxpr/anb,antd->btd/dot_general | solution.py:55
  213.8 5.1 %fusion.140 = bf16[5,16,64,128]{3,1,2,0:T(8,128)(2,1)} fusion(bf16[5,16,64,128]{3,1,2,0:T(8,128)(2,1)} %get-tuple-element.342, s32[]{:T(128)S(6)} %copy.142, f32[16,8,64,128]{3,2,1,0:T(8,128)S(1)} %bitcast.177, s32[16,8]{0,1:T(8,128)S(1)} %copy.132), kind=kOutput, calls=%fused_computation.28.clone.1 | convolution fusion | flops 201459712 | bytes 4456964 | tf_op jit(solution)/shard_map/while/body/eval_jaxpr/anb,antd->btd/dot_general | solution.py:61
  224.3 4.0 broadcast_select_fusion.6
  230.9 3.6 fusion.136
  240.9 7.3 %fusion.138 = bf16[5,16,64,128]{3,1,2,0:T(8,128)(2,1)} fusion(bf16[5,16,64,128]{3,1,2,0:T(8,128)(2,1)} %get-tuple-element.341, s32[]{:T(128)S(6)} %copy.142, f32[16,8,64,128]{3,2,1,0:T(8,128)} %bitcast.172, s32[16,8]{0,1:T(8,128)S(1)} %copy.132), kind=kOutput, calls=%fused_computation.26.clone.1 | convolution fusion | flops 201459712 | bytes 4456964 | tf_op jit(solution)/shard_map/while/body/eval_jaxpr/anb,antd->btd/dot_general | solution.py:55
  250.1 5.1 %fusion.140 = bf16[5,16,64,128]{3,1,2,0:T(8,128)(2,1)} fusion(bf16[5,16,64,128]{3,1,2,0:T(8,128)(2,1)} %get-tuple-element.342, s32[]{:T(128)S(6)} %copy.142, f32[16,8,64,128]{3,2,1,0:T(8,128)S(1)} %bitcast.177, s32[16,8]{0,1:T(8,128)S(1)} %copy.132), kind=kOutput, calls=%fused_computation.28.clone.1 | convolution fusion | flops 201459712 | bytes 4456964 | tf_op jit(solution)/shard_map/while/body/eval_jaxpr/anb,antd->btd/dot_general | solution.py:61
  260.7 4.0 broadcast_select_fusion.6
  277.3 7.2 %fusion.138 = bf16[5,16,64,128]{3,1,2,0:T(8,128)(2,1)} fusion(bf16[5,16,64,128]{3,1,2,0:T(8,128)(2,1)} %get-tuple-element.341, s32[]{:T(128)S(6)} %copy.142, f32[16,8,64,128]{3,2,1,0:T(8,128)} %bitcast.172, s32[16,8]{0,1:T(8,128)S(1)} %copy.132), kind=kOutput, calls=%fused_computation.26.clone.1 | convolution fusion | flops 201459712 | bytes 4456964 | tf_op jit(solution)/shard_map/while/body/eval_jaxpr/anb,antd->btd/dot_general | solution.py:55
  286.5 5.1 %fusion.140 = bf16[5,16,64,128]{3,1,2,0:T(8,128)(2,1)} fusion(bf16[5,16,64,128]{3,1,2,0:T(8,128)(2,1)} %get-tuple-element.342, s32[]{:T(128)S(6)} %copy.142, f32[16,8,64,128]{3,2,1,0:T(8,128)S(1)} %bitcast.177, s32[16,8]{0,1:T(8,128)S(1)} %copy.132), kind=kOutput, calls=%fused_computation.28.clone.1 | convolution fusion | flops 201459712 | bytes 4456964 | tf_op jit(solution)/shard_map/while/body/eval_jaxpr/anb,antd->btd/dot_general | solution.py:61
  297.1 4.0 broadcast_select_fusion.6
  313.7 7.3 %fusion.138 = bf16[5,16,64,128]{3,1,2,0:T(8,128)(2,1)} fusion(bf16[5,16,64,128]{3,1,2,0:T(8,128)(2,1)} %get-tuple-element.341, s32[]{:T(128)S(6)} %copy.142, f32[16,8,64,128]{3,2,1,0:T(8,128)} %bitcast.172, s32[16,8]{0,1:T(8,128)S(1)} %copy.132), kind=kOutput, calls=%fused_computation.26.clone.1 | convolution fusion | flops 201459712 | bytes 4456964 | tf_op jit(solution)/shard_map/while/body/eval_jaxpr/anb,antd->btd/dot_general | solution.py:55
  322.9 5.2 %fusion.140 = bf16[5,16,64,128]{3,1,2,0:T(8,128)(2,1)} fusion(bf16[5,16,64,128]{3,1,2,0:T(8,128)(2,1)} %get-tuple-element.342, s32[]{:T(128)S(6)} %copy.142, f32[16,8,64,128]{3,2,1,0:T(8,128)S(1)} %bitcast.177, s32[16,8]{0,1:T(8,128)S(1)} %copy.132), kind=kOutput, calls=%fused_computation.28.clone.1 | convolution fusion | flops 201459712 | bytes 4456964 | tf_op jit(solution)/shard_map/while/body/eval_jaxpr/anb,antd->btd/dot_general | solution.py:61
  333.5 4.0 broadcast_select_fusion.6
  340.1 3.6 fusion.136
  350.1 7.3 %fusion.138 = bf16[5,16,64,128]{3,1,2,0:T(8,128)(2,1)} fusion(bf16[5,16,64,128]{3,1,2,0:T(8,128)(2,1)} %get-tuple-element.341, s32[]{:T(128)S(6)} %copy.142, f32[16,8,64,128]{3,2,1,0:T(8,128)} %bitcast.172, s32[16,8]{0,1:T(8,128)S(1)} %copy.132), kind=kOutput, calls=%fused_computation.26.clone.1 | convolution fusion | flops 201459712 | bytes 4456964 | tf_op jit(solution)/shard_map/while/body/eval_jaxpr/anb,antd->btd/dot_general | solution.py:55
  359.3 5.2 %fusion.140 = bf16[5,16,64,128]{3,1,2,0:T(8,128)(2,1)} fusion(bf16[5,16,64,128]{3,1,2,0:T(8,128)(2,1)} %get-tuple-element.342, s32[]{:T(128)S(6)} %copy.142, f32[16,8,64,128]{3,2,1,0:T(8,128)S(1)} %bitcast.177, s32[16,8]{0,1:T(8,128)S(1)} %copy.132), kind=kOutput, calls=%fused_computation.28.clone.1 | convolution fusion | flops 201459712 | bytes 4456964 | tf_op jit(solution)/shard_map/while/body/eval_jaxpr/anb,antd->btd/dot_general | solution.py:61
  367.0 11.5 %fusion.68 = bf16[5120,640]{0,1:T(8,128)(2,1)} fusion(bf16[1024,5120]{1,0:T(8,128)(2,1)} %all-gather.3.cloned.1.call-done, bf16[128,8,5,128]{3,2,1,0:T(8,128)(2,1)S(1)} %bitcast.191), kind=kOutput, calls=%fused_computation.66 | convolution fusion | flops 6717440000 | bytes 18350080 | tf_op jit(solution)/shard_map/td,te->de/dot_general | solution.py:113
  378.5 9.5 %copy.97 = bf16[5120,640]{1,0:T(8,128)(2,1)} copy(bf16[5120,640]{0,1:T(8,128)(2,1)} %fusion.68) | data formatting | bytes 13107200
  392.8 4.0 all-to-all-start.3
  406.2 8.4 %all-to-all-done.3 = bf16[4,256,640]{2,1,0:T(8,128)(2,1)S(1)} async-done(((bf16[4,256,640]{2,1,0:T(8,128)(2,1)}), bf16[4,256,640]{2,1,0:T(8,128)(2,1)S(1)}, u32[]{:S(2)}, u32[]{:S(2)}) %all-to-all-start.3) | async-done | bytes 1310752 | tf_op jit(solution)/shard_map/all_to_all | solution.py:121
  415.7 3.8 all-to-all-start.4
  432.7 3.7 all-to-all-done.4
  459.3 16.6 %reduce-scatter.4.cloned.1.call-done = bf16[160,640]{1,0:T(8,128)(2,1)} async-done(((bf16[5120,640]{1,0:T(8,128)(2,1)}), bf16[160,640]{1,0:T(8,128)(2,1)}) %reduce-scatter.4.cloned.1.call-update) | async-done | bytes 204816
  (232 shorter events, 182.6 us)
Async XLA Ops:
  7.2 52.7 %copy-start = (s32[1,16]{1,0:T(1,128)S(1)}, s32[1,16]{1,0:T(1,128)}, u32[]{:S(2)}) copy-start(s32[1,16]{1,0:T(1,128)} %param.19) | copy-start | bytes 196
  7.2 73.1 %all-gather.5.cloned.1.call-start = ((), (), s32[]{:S(2)}) async-start(), calls=%async_computation.8 | async-start | bytes 6758400 | tf_op jit(solution)/shard_map/all_gather | solution.py:91
  7.9 155.8 %all-gather.3.cloned.1.call-start = ((), (), s32[]{:S(2)}) async-start(), calls=%async_computation.7 | async-start | bytes 13107200 | tf_op jit(solution)/shard_map/all_gather | solution.py:88
  12.3 22.5 %all-to-all-start = ((bf16[256,4,640]{2,0,1:T(8,128)(2,1)}), bf16[256,4,640]{2,0,1:T(8,128)(2,1)S(1)}, u32[]{:S(2)}, u32[]{:S(2)}) async-start(bf16[256,4,640]{2,0,1:T(8,128)(2,1)} %copy.73), calls=%async_computation | async-start | bytes 2621440 | tf_op jit(solution)/shard_map/all_to_all | solution.py:84
  18.4 4.9 %copy-start.5 = (bf16[256,2560]{0,1:T(8,128)(2,1)}, bf16[256,2560]{0,1:T(8,128)(2,1)S(1)}, u32[]{:S(2)}) copy-start(bf16[256,2560]{0,1:T(8,128)(2,1)S(1)} %copy.74) | copy-start | bytes 3932164
  19.4 3.9 copy-start.21
  34.7 20.5 %all-to-all-start.1 = ((bf16[256,4,640]{2,0,1:T(8,128)(2,1)}), bf16[256,4,640]{2,0,1:T(8,128)(2,1)S(1)}, u32[]{:S(2)}, u32[]{:S(2)}) async-start(bf16[256,4,640]{2,0,1:T(8,128)(2,1)} %copy.75), calls=%async_computation.1 | async-start | bytes 2621440 | tf_op jit(solution)/shard_map/all_to_all | solution.py:85
  38.3 21.4 %copy-start.20 = (s32[16,8]{0,1:T(8,128)S(1)}, s32[16,8]{0,1:T(8,128)}, u32[]{:S(2)}) copy-start(s32[16,8]{0,1:T(8,128)} %param.18) | copy-start | bytes 1540
  55.2 5.9 %copy-start.11 = (bf16[256,4,640]{2,0,1:T(8,128)(2,1)}, bf16[256,4,640]{2,0,1:T(8,128)(2,1)S(1)}, u32[]{:S(2)}) copy-start(bf16[256,4,640]{2,0,1:T(8,128)(2,1)S(1)} %all-to-all-done.1) | copy-start | bytes 3932164
  55.2 20.5 %all-to-all-start.2 = ((bf16[256,4,640]{2,0,1:T(8,128)(2,1)}), bf16[256,4,640]{2,0,1:T(8,128)(2,1)}, u32[]{:S(2)}, u32[]{:S(2)}) async-start(bf16[256,4,640]{2,0,1:T(8,128)(2,1)} %bitcast.186), calls=%async_computation.2 | async-start | bytes 2621440 | tf_op jit(solution)/shard_map/all_to_all | solution.py:86
  59.6 416.4 %reduce-scatter.4.cloned.1.call-start = ((), (), s32[]{:S(2)}) async-start(), calls=%async_computation.9 | async-start | bytes 6758400
  194.5 3.6 copy-start.2
  194.5 3.6 copy-start.3
  204.6 7.3 %copy-start.4 = (f32[16,64,512]{2,1,0:T(8,128)S(1)}, f32[16,64,512]{2,1,0:T(8,128)}, u32[]{:S(2)}) copy-start(f32[16,64,512]{2,1,0:T(8,128)} %get-tuple-element.322) | copy-start | bytes 6291460 | tf_op jit(solution)/shard_map/while
  230.9 3.6 copy-start.2
  230.9 3.6 copy-start.3
  240.9 7.3 %copy-start.4 = (f32[16,64,512]{2,1,0:T(8,128)S(1)}, f32[16,64,512]{2,1,0:T(8,128)}, u32[]{:S(2)}) copy-start(f32[16,64,512]{2,1,0:T(8,128)} %get-tuple-element.322) | copy-start | bytes 6291460 | tf_op jit(solution)/shard_map/while
  267.3 3.6 copy-start.2
  267.3 3.6 copy-start.3
  277.3 7.3 %copy-start.4 = (f32[16,64,512]{2,1,0:T(8,128)S(1)}, f32[16,64,512]{2,1,0:T(8,128)}, u32[]{:S(2)}) copy-start(f32[16,64,512]{2,1,0:T(8,128)} %get-tuple-element.322) | copy-start | bytes 6291460 | tf_op jit(solution)/shard_map/while
  303.6 3.6 copy-start.2
  303.6 3.6 copy-start.3
  313.7 7.3 %copy-start.4 = (f32[16,64,512]{2,1,0:T(8,128)S(1)}, f32[16,64,512]{2,1,0:T(8,128)}, u32[]{:S(2)}) copy-start(f32[16,64,512]{2,1,0:T(8,128)} %get-tuple-element.322) | copy-start | bytes 6291460 | tf_op jit(solution)/shard_map/while
  340.1 3.6 copy-start.2
  340.1 3.6 copy-start.3
  350.1 7.3 %copy-start.4 = (f32[16,64,512]{2,1,0:T(8,128)S(1)}, f32[16,64,512]{2,1,0:T(8,128)}, u32[]{:S(2)}) copy-start(f32[16,64,512]{2,1,0:T(8,128)} %get-tuple-element.322) | copy-start | bytes 6291460 | tf_op jit(solution)/shard_map/while
  392.8 21.9 %all-to-all-start.3 = ((bf16[4,256,640]{2,1,0:T(8,128)(2,1)}), bf16[4,256,640]{2,1,0:T(8,128)(2,1)S(1)}, u32[]{:S(2)}, u32[]{:S(2)}) async-start(bf16[4,256,640]{2,1,0:T(8,128)(2,1)} %all_to_all.79), calls=%async_computation.3 | async-start | bytes 2621440 | tf_op jit(solution)/shard_map/all_to_all | solution.py:121
  415.7 20.7 %all-to-all-start.4 = ((bf16[4,256,640]{2,1,0:T(8,128)(2,1)}), bf16[4,256,640]{2,1,0:T(8,128)(2,1)S(1)}, u32[]{:S(2)}, u32[]{:S(2)}) async-start(bf16[4,256,640]{2,1,0:T(8,128)(2,1)} %all_to_all.81), calls=%async_computation.4 | async-start | bytes 2621440 | tf_op jit(solution)/shard_map/all_to_all | solution.py:122
  437.5 19.6 %all-to-all-start.5 = ((bf16[4,256,640]{2,1,0:T(8,128)(2,1)}), bf16[4,256,640]{2,1,0:T(8,128)(2,1)S(1)}, u32[]{:S(2)}, u32[]{:S(2)}) async-start(bf16[4,256,640]{2,1,0:T(8,128)(2,1)} %all_to_all.83), calls=%async_computation.5 | async-start | bytes 2621440 | tf_op jit(solution)/shard_map/all_to_all | solution.py:123
  444.0 3.4 copy-start.6
  444.0 3.4 copy-start.19
  457.1 20.8 %copy-start.1 = (s32[1,16]{1,0:T(1,128)S(1)}, s32[1,16]{1,0:T(1,128)}, u32[]{:S(2)}) copy-start(s32[1,16]{1,0:T(1,128)} %param.19) | copy-start | bytes 196
  (16 other events, 34.8 us)
Sparse Core Ops, SparseCore 0:
  10.3 52.1 all-gather.4
  64.1 99.5 all-gather.2
  388.1 87.7 reduce-scatter.3
where the time goes:
time: 494 us; the launch traced here: 485 us
  matrix products  156 us (32%)
  waiting for transfers between devices  151 us (31%)
  local copies, waits for them, and re-layouts  98.8 us (20%)
  other arithmetic  40.3 us (8%)
  starting transfers between devices  23.8 us (5%)
  between operations  14.3 us (3%)
    all_gather x1, waiting for transfers between devices, per_device(): cot_all = lax.all_gather(out_grad, 'seq', axis=0, tiled=True)  83.5 us
    dot_general x25, matrix products, multiply(): return jnp.einsum(pattern, left, right, preferred_element_type=jnp.float32)  57.5 us
    dot_general x5, matrix products, tile_attention(): jnp.einsum('anb,antd->btd', owners, grad_key_near.reshape(tile_count, nei...  36.3 us
    dot_general x5, matrix products, tile_attention(): jnp.einsum('anb,antd->btd', owners, grad_value_near.reshape(tile_count, n...  25.7 us
    unnamed x56, local copies, waits for them, and re-layouts  24 us
    select_n x5, other arithmetic, tile_attention(): jnp.take(key_tiles, tile_pairs, axis=0)  20.2 us
    unnamed x4, waiting for transfers between devices  18 us
    all_to_all x1, waiting for transfers between devices, per_device(): lax.all_to_all(key_normed, 'seq', split_axis=1, concat_axis=0, tiled=True)  14.4 us
  transfers between devices with their start and end apart: 9, of which 8 were waited for; matrix products, arithmetic and copies ran while one was open for 12% of the time, Pallas kernels for 0%

commit v1 on v0

--- a/solution.py
+++ b/solution.py
@@ -81,7 +81,12 @@
     query_normed, query_scale = normalize(queries, gain_q)
     key_normed, key_scale = normalize(keys, gain_k)
     query_heads, key_heads, value_heads = (
-        lax.all_to_all(query_normed, "seq", split_axis=1, concat_axis=0, tiled=True),
+        jnp.concatenate(
+            lax.all_to_all(
+                jnp.stack(jnp.split(query_normed, lax.axis_size("seq"), axis=1)), "seq", 0, 0
+            ),
+            axis=0,
+        ),
         lax.all_to_all(key_normed, "seq", split_axis=1, concat_axis=0, tiled=True),
         lax.all_to_all(values, "seq", split_axis=1, concat_axis=0, tiled=True),
     )

time: 494 us -> 494 us (level)
    reshape x4 -> x3, local copies, waits for them, and re-layouts: 10.8 us -> 9.36 us  [split(): field.reshape(tile_count, tile_rows, head_count, HEAD_DIM)]
  transfers between devices with their start and end apart: 9 -> 9, of which waited for: 8 -> 8; matrix products, arithmetic and copies ran while one was open for 12% -> 13% of each run, Pallas kernels for 0% -> 0%
where the time goes in v1:
time: 494 us; the launch traced here: 485 us
  matrix products  156 us (32%)
  waiting for transfers between devices  147 us (30%)
  local copies, waits for them, and re-layouts  101 us (20%)
  other arithmetic  41.6 us (8%)
  starting transfers between devices  23.8 us (5%)
  between operations  14.3 us (3%)
    all_gather x1, waiting for transfers between devices, per_device(): cot_all = lax.all_gather(out_grad, 'seq', axis=0, tiled=True)  83.6 us
    dot_general x25, matrix products, multiply(): return jnp.einsum(pattern, left, right, preferred_element_type=jnp.float32)  57.5 us
    dot_general x5, matrix products, tile_attention(): jnp.einsum('anb,antd->btd', owners, grad_key_near.reshape(tile_count, nei...  36.3 us
    dot_general x5, matrix products, tile_attention(): jnp.einsum('anb,antd->btd', owners, grad_value_near.reshape(tile_count, n...  25.7 us
    unnamed x56, local copies, waits for them, and re-layouts  24 us
    select_n x5, other arithmetic, tile_attention(): jnp.take(key_tiles, tile_pairs, axis=0)  20.1 us
    unnamed x4, waiting for transfers between devices  18 us
    all_to_all x1, waiting for transfers between devices, per_device(): lax.all_to_all(key_normed, 'seq', split_axis=1, concat_axis=0, tiled=True)  14.4 us
  transfers between devices with their start and end apart: 9, of which 8 were waited for; matrix products, arithmetic and copies ran while one was open for 13% of the time, Pallas kernels for 0%

profile of v1, /device:TPU:0, one launch (start us, length us, event | category | flops | bytes accessed | tf_op | source)
XLA Modules:
  0.0 484.8 jit_solution(10376774502786844932)
XLA Ops:
  12.1 4.5 all-to-all-start
  23.3 11.3 %all-to-all-done = bf16[4,256,640]{1,2,0:T(8,128)(2,1)S(1)} async-done(((bf16[4,256,640]{1,2,0:T(8,128)(2,1)}), bf16[4,256,640]{1,2,0:T(8,128)(2,1)S(1)}, u32[]{:S(2)}, u32[]{:S(2)}) %all-to-all-start) | async-done | bytes 1310752 | tf_op jit(solution)/shard_map/all_to_all | solution.py:85
  40.6 14.4 %all-to-all-done.1 = bf16[256,4,640]{2,0,1:T(8,128)(2,1)S(1)} async-done(((bf16[256,4,640]{2,0,1:T(8,128)(2,1)}), bf16[256,4,640]{2,0,1:T(8,128)(2,1)S(1)}, u32[]{:S(2)}, u32[]{:S(2)}) %all-to-all-start.1) | async-done | bytes 1310752 | tf_op jit(solution)/shard_map/all_to_all | solution.py:90
  55.1 4.3 all-to-all-start.2
  70.5 5.0 %all-to-all-done.2 = bf16[256,4,640]{2,0,1:T(8,128)(2,1)} async-done(((bf16[256,4,640]{2,0,1:T(8,128)(2,1)}), bf16[256,4,640]{2,0,1:T(8,128)(2,1)}, u32[]{:S(2)}, u32[]{:S(2)}) %all-to-all-start.2) | async-done | bytes 1310752 | tf_op jit(solution)/shard_map/all_to_all | solution.py:91
  80.1 83.6 %all-gather.3.cloned.1.call-done = bf16[1024,5120]{1,0:T(8,128)(2,1)} async-done(((bf16[256,5120]{1,0:T(8,128)(2,1)}), bf16[1024,5120]{1,0:T(8,128)(2,1)}) %all-gather.3.cloned.1.call-update) | async-done | bytes 10485776 | tf_op jit(solution)/shard_map/all_gather | solution.py:93
  163.8 13.8 %convolution_convert_fusion.1 = bf16[1024,640]{1,0:T(8,128)(2,1)} fusion(bf16[1024,5120]{1,0:T(8,128)(2,1)} %all-gather.3.cloned.1.call-done, bf16[5120,640]{1,0:T(8,128)(2,1)} %all-gather.5.cloned.1.call-done), kind=kOutput, calls=%fused_computation.95 | convolution fusion | flops 6711541760 | bytes 18350080 | tf_op jit(solution)/shard_map/dot_general | solution.py:95
  182.1 182.5 %while.18 = (s32[]{:T(128)}, bf16[5,16,64,128]{3,2,1,0:T(8,128)(2,1)}, bf16[5,16,64,128]{3,2,1,0:T(8,128)(2,1)}, bf16[5,16,64,128]{3,1,2,0:T(8,128)(2,1)}, bf16[...) while((s32[]{:T(128)}, ...), condition=%wide.region_6.8_spmd, body=%wide.region_2.7_spmd.sunk | while | flops 1219638656 | bytes 88276472 | solution.py:108
  188.0 4.0 broadcast_select_fusion.6
  204.6 7.3 %fusion.138 = bf16[5,16,64,128]{3,1,2,0:T(8,128)(2,1)} fusion(bf16[5,16,64,128]{3,1,2,0:T(8,128)(2,1)} %get-tuple-element.345, s32[]{:T(128)S(6)} %copy.142, f32[16,8,64,128]{3,2,1,0:T(8,128)} %bitcast.178, s32[16,8]{0,1:T(8,128)S(1)} %copy.132), kind=kOutput, calls=%fused_computation.26.clone.1 | convolution fusion | flops 201459712 | bytes 4456964 | tf_op jit(solution)/shard_map/while/body/eval_jaxpr/anb,antd->btd/dot_general | solution.py:55
  213.8 5.1 %fusion.140 = bf16[5,16,64,128]{3,1,2,0:T(8,128)(2,1)} fusion(bf16[5,16,64,128]{3,1,2,0:T(8,128)(2,1)} %get-tuple-element.346, s32[]{:T(128)S(6)} %copy.142, f32[16,8,64,128]{3,2,1,0:T(8,128)S(1)} %bitcast.183, s32[16,8]{0,1:T(8,128)S(1)} %copy.132), kind=kOutput, calls=%fused_computation.28.clone.1 | convolution fusion | flops 201459712 | bytes 4456964 | tf_op jit(solution)/shard_map/while/body/eval_jaxpr/anb,antd->btd/dot_general | solution.py:61
  224.3 4.0 broadcast_select_fusion.6
  240.9 7.3 %fusion.138 = bf16[5,16,64,128]{3,1,2,0:T(8,128)(2,1)} fusion(bf16[5,16,64,128]{3,1,2,0:T(8,128)(2,1)} %get-tuple-element.345, s32[]{:T(128)S(6)} %copy.142, f32[16,8,64,128]{3,2,1,0:T(8,128)} %bitcast.178, s32[16,8]{0,1:T(8,128)S(1)} %copy.132), kind=kOutput, calls=%fused_computation.26.clone.1 | convolution fusion | flops 201459712 | bytes 4456964 | tf_op jit(solution)/shard_map/while/body/eval_jaxpr/anb,antd->btd/dot_general | solution.py:55
  250.1 5.1 %fusion.140 = bf16[5,16,64,128]{3,1,2,0:T(8,128)(2,1)} fusion(bf16[5,16,64,128]{3,1,2,0:T(8,128)(2,1)} %get-tuple-element.346, s32[]{:T(128)S(6)} %copy.142, f32[16,8,64,128]{3,2,1,0:T(8,128)S(1)} %bitcast.183, s32[16,8]{0,1:T(8,128)S(1)} %copy.132), kind=kOutput, calls=%fused_computation.28.clone.1 | convolution fusion | flops 201459712 | bytes 4456964 | tf_op jit(solution)/shard_map/while/body/eval_jaxpr/anb,antd->btd/dot_general | solution.py:61
  260.7 4.0 broadcast_select_fusion.6
  267.2 3.6 fusion.136
  277.3 7.3 %fusion.138 = bf16[5,16,64,128]{3,1,2,0:T(8,128)(2,1)} fusion(bf16[5,16,64,128]{3,1,2,0:T(8,128)(2,1)} %get-tuple-element.345, s32[]{:T(128)S(6)} %copy.142, f32[16,8,64,128]{3,2,1,0:T(8,128)} %bitcast.178, s32[16,8]{0,1:T(8,128)S(1)} %copy.132), kind=kOutput, calls=%fused_computation.26.clone.1 | convolution fusion | flops 201459712 | bytes 4456964 | tf_op jit(solution)/shard_map/while/body/eval_jaxpr/anb,antd->btd/dot_general | solution.py:55
  286.5 5.1 %fusion.140 = bf16[5,16,64,128]{3,1,2,0:T(8,128)(2,1)} fusion(bf16[5,16,64,128]{3,1,2,0:T(8,128)(2,1)} %get-tuple-element.346, s32[]{:T(128)S(6)} %copy.142, f32[16,8,64,128]{3,2,1,0:T(8,128)S(1)} %bitcast.183, s32[16,8]{0,1:T(8,128)S(1)} %copy.132), kind=kOutput, calls=%fused_computation.28.clone.1 | convolution fusion | flops 201459712 | bytes 4456964 | tf_op jit(solution)/shard_map/while/body/eval_jaxpr/anb,antd->btd/dot_general | solution.py:61
  297.1 4.0 broadcast_select_fusion.6
  303.6 3.6 fusion.136
  313.7 7.3 %fusion.138 = bf16[5,16,64,128]{3,1,2,0:T(8,128)(2,1)} fusion(bf16[5,16,64,128]{3,1,2,0:T(8,128)(2,1)} %get-tuple-element.345, s32[]{:T(128)S(6)} %copy.142, f32[16,8,64,128]{3,2,1,0:T(8,128)} %bitcast.178, s32[16,8]{0,1:T(8,128)S(1)} %copy.132), kind=kOutput, calls=%fused_computation.26.clone.1 | convolution fusion | flops 201459712 | bytes 4456964 | tf_op jit(solution)/shard_map/while/body/eval_jaxpr/anb,antd->btd/dot_general | solution.py:55
  322.9 5.2 %fusion.140 = bf16[5,16,64,128]{3,1,2,0:T(8,128)(2,1)} fusion(bf16[5,16,64,128]{3,1,2,0:T(8,128)(2,1)} %get-tuple-element.346, s32[]{:T(128)S(6)} %copy.142, f32[16,8,64,128]{3,2,1,0:T(8,128)S(1)} %bitcast.183, s32[16,8]{0,1:T(8,128)S(1)} %copy.132), kind=kOutput, calls=%fused_computation.28.clone.1 | convolution fusion | flops 201459712 | bytes 4456964 | tf_op jit(solution)/shard_map/while/body/eval_jaxpr/anb,antd->btd/dot_general | solution.py:61
  333.5 4.0 broadcast_select_fusion.6
  350.1 7.3 %fusion.138 = bf16[5,16,64,128]{3,1,2,0:T(8,128)(2,1)} fusion(bf16[5,16,64,128]{3,1,2,0:T(8,128)(2,1)} %get-tuple-element.345, s32[]{:T(128)S(6)} %copy.142, f32[16,8,64,128]{3,2,1,0:T(8,128)} %bitcast.178, s32[16,8]{0,1:T(8,128)S(1)} %copy.132), kind=kOutput, calls=%fused_computation.26.clone.1 | convolution fusion | flops 201459712 | bytes 4456964 | tf_op jit(solution)/shard_map/while/body/eval_jaxpr/anb,antd->btd/dot_general | solution.py:55
  359.3 5.2 %fusion.140 = bf16[5,16,64,128]{3,1,2,0:T(8,128)(2,1)} fusion(bf16[5,16,64,128]{3,1,2,0:T(8,128)(2,1)} %get-tuple-element.346, s32[]{:T(128)S(6)} %copy.142, f32[16,8,64,128]{3,2,1,0:T(8,128)S(1)} %bitcast.183, s32[16,8]{0,1:T(8,128)S(1)} %copy.132), kind=kOutput, calls=%fused_computation.28.clone.1 | convolution fusion | flops 201459712 | bytes 4456964 | tf_op jit(solution)/shard_map/while/body/eval_jaxpr/anb,antd->btd/dot_general | solution.py:61
  367.0 11.5 %fusion.68 = bf16[5120,640]{0,1:T(8,128)(2,1)} fusion(bf16[1024,5120]{1,0:T(8,128)(2,1)} %all-gather.3.cloned.1.call-done, bf16[128,8,5,128]{3,2,1,0:T(8,128)(2,1)S(1)} %bitcast.195), kind=kOutput, calls=%fused_computation.66 | convolution fusion | flops 6717440000 | bytes 18350080 | tf_op jit(solution)/shard_map/td,te->de/dot_general | solution.py:118
  378.5 9.5 %copy.97 = bf16[5120,640]{1,0:T(8,128)(2,1)} copy(bf16[5120,640]{0,1:T(8,128)(2,1)} %fusion.68) | data formatting | bytes 13107200
  392.8 4.0 all-to-all-start.3
  406.3 8.4 %all-to-all-done.3 = bf16[4,256,640]{2,1,0:T(8,128)(2,1)S(1)} async-done(((bf16[4,256,640]{2,1,0:T(8,128)(2,1)}), bf16[4,256,640]{2,1,0:T(8,128)(2,1)S(1)}, u32[]{:S(2)}, u32[]{:S(2)}) %all-to-all-start.3) | async-done | bytes 1310752 | tf_op jit(solution)/shard_map/all_to_all | solution.py:126
  415.8 3.8 all-to-all-start.4
  432.7 3.7 all-to-all-done.4
  459.4 16.6 %reduce-scatter.4.cloned.1.call-done = bf16[160,640]{1,0:T(8,128)(2,1)} async-done(((bf16[5120,640]{1,0:T(8,128)(2,1)}), bf16[160,640]{1,0:T(8,128)(2,1)}) %reduce-scatter.4.cloned.1.call-update) | async-done | bytes 204816
  (234 shorter events, 185.7 us)
Async XLA Ops:
  7.2 52.6 %copy-start = (s32[1,16]{1,0:T(1,128)S(1)}, s32[1,16]{1,0:T(1,128)}, u32[]{:S(2)}) copy-start(s32[1,16]{1,0:T(1,128)} %param.19) | copy-start | bytes 196
  7.2 72.9 %all-gather.5.cloned.1.call-start = ((), (), s32[]{:S(2)}) async-start(), calls=%async_computation.8 | async-start | bytes 6758400 | tf_op jit(solution)/shard_map/all_gather | solution.py:96
  7.9 155.8 %all-gather.3.cloned.1.call-start = ((), (), s32[]{:S(2)}) async-start(), calls=%async_computation.7 | async-start | bytes 13107200 | tf_op jit(solution)/shard_map/all_gather | solution.py:93
  12.1 22.5 %all-to-all-start = ((bf16[4,256,640]{1,2,0:T(8,128)(2,1)}), bf16[4,256,640]{1,2,0:T(8,128)(2,1)S(1)}, u32[]{:S(2)}, u32[]{:S(2)}) async-start(bf16[4,256,640]{1,2,0:T(8,128)(2,1)} %pad_maximum_fusion), calls=%async_computation | async-start | bytes 2621440 | tf_op jit(solution)/shard_map/all_to_all | solution.py:85
  18.3 5.0 %copy-start.7 = (bf16[256,2560]{0,1:T(8,128)(2,1)}, bf16[256,2560]{0,1:T(8,128)(2,1)S(1)}, u32[]{:S(2)}) copy-start(bf16[256,2560]{0,1:T(8,128)(2,1)S(1)} %copy.74) | copy-start | bytes 3932164
  34.6 20.5 %all-to-all-start.1 = ((bf16[256,4,640]{2,0,1:T(8,128)(2,1)}), bf16[256,4,640]{2,0,1:T(8,128)(2,1)S(1)}, u32[]{:S(2)}, u32[]{:S(2)}) async-start(bf16[256,4,640]{2,0,1:T(8,128)(2,1)} %copy.75), calls=%async_computation.1 | async-start | bytes 2621440 | tf_op jit(solution)/shard_map/all_to_all | solution.py:90
  38.1 21.4 %copy-start.20 = (s32[16,8]{0,1:T(8,128)S(1)}, s32[16,8]{0,1:T(8,128)}, u32[]{:S(2)}) copy-start(s32[16,8]{0,1:T(8,128)} %param.18) | copy-start | bytes 1540
  55.1 5.9 %copy-start.11 = (bf16[256,4,640]{2,0,1:T(8,128)(2,1)}, bf16[256,4,640]{2,0,1:T(8,128)(2,1)S(1)}, u32[]{:S(2)}) copy-start(bf16[256,4,640]{2,0,1:T(8,128)(2,1)S(1)} %all-to-all-done.1) | copy-start | bytes 3932164
  55.1 20.5 %all-to-all-start.2 = ((bf16[256,4,640]{2,0,1:T(8,128)(2,1)}), bf16[256,4,640]{2,0,1:T(8,128)(2,1)}, u32[]{:S(2)}, u32[]{:S(2)}) async-start(bf16[256,4,640]{2,0,1:T(8,128)(2,1)} %bitcast.191), calls=%async_computation.2 | async-start | bytes 2621440 | tf_op jit(solution)/shard_map/all_to_all | solution.py:91
  59.4 416.6 %reduce-scatter.4.cloned.1.call-start = ((), (), s32[]{:S(2)}) async-start(), calls=%async_computation.9 | async-start | bytes 6758400
  194.5 3.6 copy-start.2
  194.5 3.6 copy-start.3
  204.6 7.3 %copy-start.4 = (f32[16,64,512]{2,1,0:T(8,128)S(1)}, f32[16,64,512]{2,1,0:T(8,128)}, u32[]{:S(2)}) copy-start(f32[16,64,512]{2,1,0:T(8,128)} %get-tuple-element.326) | copy-start | bytes 6291460 | tf_op jit(solution)/shard_map/while
  230.9 3.6 copy-start.2
  230.9 3.6 copy-start.3
  240.9 7.3 %copy-start.4 = (f32[16,64,512]{2,1,0:T(8,128)S(1)}, f32[16,64,512]{2,1,0:T(8,128)}, u32[]{:S(2)}) copy-start(f32[16,64,512]{2,1,0:T(8,128)} %get-tuple-element.326) | copy-start | bytes 6291460 | tf_op jit(solution)/shard_map/while
  267.2 3.6 copy-start.2
  267.2 3.6 copy-start.3
  277.3 7.3 %copy-start.4 = (f32[16,64,512]{2,1,0:T(8,128)S(1)}, f32[16,64,512]{2,1,0:T(8,128)}, u32[]{:S(2)}) copy-start(f32[16,64,512]{2,1,0:T(8,128)} %get-tuple-element.326) | copy-start | bytes 6291460 | tf_op jit(solution)/shard_map/while
  303.6 3.6 copy-start.2
  303.6 3.6 copy-start.3
  313.7 7.3 %copy-start.4 = (f32[16,64,512]{2,1,0:T(8,128)S(1)}, f32[16,64,512]{2,1,0:T(8,128)}, u32[]{:S(2)}) copy-start(f32[16,64,512]{2,1,0:T(8,128)} %get-tuple-element.326) | copy-start | bytes 6291460 | tf_op jit(solution)/shard_map/while
  340.0 3.6 copy-start.2
  340.0 3.6 copy-start.3
  350.1 7.3 %copy-start.4 = (f32[16,64,512]{2,1,0:T(8,128)S(1)}, f32[16,64,512]{2,1,0:T(8,128)}, u32[]{:S(2)}) copy-start(f32[16,64,512]{2,1,0:T(8,128)} %get-tuple-element.326) | copy-start | bytes 6291460 | tf_op jit(solution)/shard_map/while
  392.8 21.9 %all-to-all-start.3 = ((bf16[4,256,640]{2,1,0:T(8,128)(2,1)}), bf16[4,256,640]{2,1,0:T(8,128)(2,1)S(1)}, u32[]{:S(2)}, u32[]{:S(2)}) async-start(bf16[4,256,640]{2,1,0:T(8,128)(2,1)} %all_to_all.68), calls=%async_computation.3 | async-start | bytes 2621440 | tf_op jit(solution)/shard_map/all_to_all | solution.py:126
  415.8 20.7 %all-to-all-start.4 = ((bf16[4,256,640]{2,1,0:T(8,128)(2,1)}), bf16[4,256,640]{2,1,0:T(8,128)(2,1)S(1)}, u32[]{:S(2)}, u32[]{:S(2)}) async-start(bf16[4,256,640]{2,1,0:T(8,128)(2,1)} %all_to_all.70), calls=%async_computation.4 | async-start | bytes 2621440 | tf_op jit(solution)/shard_map/all_to_all | solution.py:127
  422.6 3.4 copy-start.17
  437.5 19.6 %all-to-all-start.5 = ((bf16[4,256,640]{2,1,0:T(8,128)(2,1)}), bf16[4,256,640]{2,1,0:T(8,128)(2,1)S(1)}, u32[]{:S(2)}, u32[]{:S(2)}) async-start(bf16[4,256,640]{2,1,0:T(8,128)(2,1)} %all_to_all.72), calls=%async_computation.5 | async-start | bytes 2621440 | tf_op jit(solution)/shard_map/all_to_all | solution.py:128
  444.0 3.4 copy-start.8
  444.0 3.4 copy-start.19
  457.1 20.9 %copy-start.1 = (s32[1,16]{1,0:T(1,128)S(1)}, s32[1,16]{1,0:T(1,128)}, u32[]{:S(2)}) copy-start(s32[1,16]{1,0:T(1,128)} %param.19) | copy-start | bytes 196
  (16 other events, 31.6 us)
Sparse Core Ops, SparseCore 0:
  10.3 52.1 all-gather.4
  64.1 99.5 all-gather.2
  388.2 87.7 reduce-scatter.3
